TPU v7x, 512 devices: a whole 4x8x8 slice. The times are simulated.
512 devices in a mesh: dp: 16 (over x, z_hi), ctx: 32 (over z_lo, y, core).
Axes of the slice: x: 4, y: 8, z: 8 (z_hi: 4, z_lo: 2; z = z_hi * 2 + z_lo), core: 2. Of those that a mesh axis runs over, the one named last changes fastest.
Arguments:
- act_input: bfloat16 [81920, 2048], P(('dp', 'ctx')), may hold values from -150 to 150
- out_grad: bfloat16 [81920, 2048], P(('dp', 'ctx')), may hold values from -150 to 150
Outputs:
- act_factor: float32 [32, 16, 16, 512], P('ctx', 'dp')
- grad_factor: float32 [32, 16, 16, 512], P('ctx', 'dp')
All inputs are finite; a program needn't handle non-finite values.
Results may differ from a plain program's by a relative error of at most 0.0003.
Values may be sent and summed in bfloat16 or wider, within the bound.
A program may use at most 64 MiB of HBM per device.

v0:
```python
import jax
import jax.numpy as jnp
from jax import lax
from jax.sharding import PartitionSpec as P

damping = 1.0


def swapped(value, axis, apart):
    return lax.ppermute(value, axis, [(i, i ^ 1 << apart) for i in range(lax.axis_size(axis))])


def outgoing(samples, row_tiles, col_tiles):
    tok_rows, feat_width = samples.shape
    quarter_rows = tok_rows // 4
    tile_rows = feat_width // row_tiles
    tile_cols = feat_width // col_tiles
    quarters = samples.reshape(4, quarter_rows, feat_width)
    row_blocks = quarters.reshape(4, quarter_rows, row_tiles, tile_rows).transpose(2, 0, 1, 3)
    row_blocks = jnp.broadcast_to(
        row_blocks[:, None], (row_tiles, col_tiles, 4, quarter_rows, tile_rows)
    )
    row_blocks = row_blocks.reshape(row_tiles * col_tiles * 4, quarter_rows, tile_rows)
    col_blocks = quarters.reshape(4, quarter_rows, col_tiles, tile_cols).transpose(2, 0, 1, 3)
    col_blocks = jnp.broadcast_to(
        col_blocks[None], (row_tiles, col_tiles, 4, quarter_rows, tile_cols)
    )
    col_blocks = col_blocks.reshape(row_tiles * col_tiles * 4, quarter_rows, tile_cols)
    return (row_blocks, col_blocks)


def tile_product(row_blocks, col_blocks, factor_scale):
    contract = (((0,), (0,)), ((), ()))
    left_side = row_blocks.reshape(-1, row_blocks.shape[2])
    right_side = col_blocks.reshape(-1, col_blocks.shape[2])
    product = lax.dot_general(left_side, right_side, contract, preferred_element_type=jnp.float32)
    return product * factor_scale


def split_halves(partial_value, owner_pos, level):
    half_rows = partial_value.shape[-2] // 2
    low_half = partial_value[..., :half_rows, :]
    top_half = partial_value[..., half_rows:, :]
    upper_side = owner_pos // (1 << level) % 2 == 1
    kept = jnp.where(upper_side, top_half, low_half)
    sent = jnp.where(upper_side, low_half, top_half)
    return (kept, sent)


def fold_pair(partial_value, owner_pos):
    for level in (1, 0):
        kept, sent = split_halves(partial_value, owner_pos, level)
        partial_value = kept + swapped(sent, "ctx", level)
    return partial_value


def on_device(act_input, out_grad):
    ctx_size = lax.axis_size("ctx")
    dp_size = lax.axis_size("dp")
    tile_count = ctx_size // 4
    row_tiles = max(1, tile_count // 4)
    col_tiles = tile_count // row_tiles
    tok_rows, feat_width = act_input.shape
    tile_rows = feat_width // row_tiles
    tile_cols = feat_width // col_tiles
    piece_rows = tile_rows // (4 * dp_size)
    factor_scale = 1.0 / (tok_rows * ctx_size * dp_size)
    ctx_pos = lax.axis_index("ctx")
    owner_pos = ctx_pos % 4
    act_rows, act_cols = outgoing(act_input, row_tiles, col_tiles)
    grad_rows, grad_cols = outgoing(out_grad, row_tiles, col_tiles)
    received = (
        lax.all_to_all(act_rows, "ctx", split_axis=0, concat_axis=0, tiled=True),
        lax.all_to_all(act_cols, "ctx", split_axis=0, concat_axis=0, tiled=True),
        lax.all_to_all(grad_rows, "ctx", split_axis=0, concat_axis=0, tiled=True),
        lax.all_to_all(grad_cols, "ctx", split_axis=0, concat_axis=0, tiled=True),
    )
    act_tile = tile_product(received[0], received[1], factor_scale)
    grad_tile = tile_product(received[2], received[3], factor_scale)
    folded = fold_pair(jnp.stack([act_tile, grad_tile]), owner_pos)
    shares = lax.psum_scatter(folded, "dp", scatter_dimension=1, tiled=True)
    act_share = shares[0]
    grad_share = shares[1]
    tile_index = ctx_pos // 4
    group_index = lax.axis_index("dp")
    first_row = (
        tile_index // col_tiles * tile_rows
        + owner_pos * (tile_rows // 4)
        + group_index * piece_rows
    )
    first_col = tile_index % col_tiles * tile_cols
    row_ids = first_row + jnp.arange(piece_rows, dtype=jnp.int32)
    col_ids = first_col + jnp.arange(tile_cols, dtype=jnp.int32)
    diag_mask = (row_ids[:, None] == col_ids[None, :]).astype(jnp.float32)
    act_trace, grad_trace = lax.psum(
        (jnp.sum(act_share * diag_mask), jnp.sum(grad_share * diag_mask)), ("dp", "ctx")
    )
    ratio = jnp.sqrt(act_trace / grad_trace)
    act_out = act_share + ratio * damping * diag_mask
    grad_out = grad_share + damping / ratio * diag_mask
    return (act_out[None, None], grad_out[None, None])


def solution(mesh):
    placed = (P(("dp", "ctx"), None), P(("dp", "ctx"), None))
    return jax.shard_map(
        on_device,
        mesh=mesh,
        in_specs=placed,
        out_specs=(P("ctx", "dp", None, None), P("ctx", "dp", None, None)),
        check_vma=False,
    )
```

profile of v0, /device:TPU:1, one launch (start us, length us, event | category | flops | bytes accessed | tf_op | source)
XLA Modules:
  0.0 495.8 jit_solution(5948330725996562143)
XLA Ops:
  7.2 2.1 reshape_reshape.15
  10.6 10.6 %all-to-all-start.3 = ((bf16[32,40,512]{2,1,0:T(8,128)(2,1)}), bf16[32,40,512]{2,1,0:T(8,128)(2,1)S(1)}, u32[]{:S(2)}, u32[]{:S(2)}) async-start(bf16[32,40,512]{2,1,0:T(8,128)(2,1)} %bitcast.9), calls=%async_computation.3 | async-start | bytes 2621440 | tf_op jit(solution)/shard_map/all_to_all | solution.py:76
  21.8 31.9 %all-to-all-done.3 = bf16[32,40,512]{2,1,0:T(8,128)(2,1)S(1)} async-done(((bf16[32,40,512]{2,1,0:T(8,128)(2,1)}), bf16[32,40,512]{2,1,0:T(8,128)(2,1)S(1)}, u32[]{:S(2)}, u32[]{:S(2)}) %all-to-all-start.3) | async-done | bytes 1310752 | tf_op jit(solution)/shard_map/all_to_all | solution.py:76
  55.2 5.6 %all-to-all-start.1 = ((bf16[32,40,512]{2,1,0:T(8,128)(2,1)}), bf16[32,40,512]{2,1,0:T(8,128)(2,1)}, u32[]{:S(2)}, u32[]{:S(2)}) async-start(bf16[32,40,512]{2,1,0:T(8,128)(2,1)} %bitcast.3), calls=%async_computation.1 | async-start | bytes 2621440 | tf_op jit(solution)/shard_map/all_to_all | solution.py:74
  61.5 32.1 %all-to-all-done.1 = bf16[32,40,512]{2,1,0:T(8,128)(2,1)} async-done(((bf16[32,40,512]{2,1,0:T(8,128)(2,1)}), bf16[32,40,512]{2,1,0:T(8,128)(2,1)}, u32[]{:S(2)}, u32[]{:S(2)}) %all-to-all-start.1) | async-done | bytes 1310752 | tf_op jit(solution)/shard_map/all_to_all | solution.py:74
  93.6 1.8 broadcast_in_dim.10
  95.4 5.5 %all-to-all-start.2 = ((bf16[32,40,1024]{2,1,0:T(8,128)(2,1)}), bf16[32,40,1024]{2,1,0:T(8,128)(2,1)S(1)}, u32[]{:S(2)}, u32[]{:S(2)}) async-start(bf16[32,40,1024]{2,1,0:T(8,128)(2,1)} %bitcast.7), calls=%async_computation.2 | async-start | bytes 5242880 | tf_op jit(solution)/shard_map/all_to_all | solution.py:75
  100.9 1.3 reshape_reshape.12
  103.5 58.3 %all-to-all-done.2 = bf16[32,40,1024]{2,1,0:T(8,128)(2,1)S(1)} async-done(((bf16[32,40,1024]{2,1,0:T(8,128)(2,1)}), bf16[32,40,1024]{2,1,0:T(8,128)(2,1)S(1)}, u32[]{:S(2)}, u32[]{:S(2)}) %all-to-all-start.2) | async-done | bytes 2621472 | tf_op jit(solution)/shard_map/all_to_all | solution.py:75
  161.8 2.0 broadcast_in_dim.8
  164.1 5.5 %all-to-all-start = ((bf16[32,40,1024]{2,1,0:T(8,128)(2,1)}), bf16[32,40,1024]{2,1,0:T(8,128)(2,1)}, u32[]{:S(2)}, u32[]{:S(2)}) async-start(bf16[32,40,1024]{2,1,0:T(8,128)(2,1)} %bitcast.1), calls=%async_computation | async-start | bytes 5242880 | tf_op jit(solution)/shard_map/all_to_all | solution.py:73
  169.7 3.7 fusion.1
  173.3 57.2 %all-to-all-done = bf16[32,40,1024]{2,1,0:T(8,128)(2,1)} async-done(((bf16[32,40,1024]{2,1,0:T(8,128)(2,1)}), bf16[32,40,1024]{2,1,0:T(8,128)(2,1)}, u32[]{:S(2)}, u32[]{:S(2)}) %all-to-all-start) | async-done | bytes 2621472 | tf_op jit(solution)/shard_map/all_to_all | solution.py:73
  230.5 3.7 fusion.2
  234.2 1.9 broadcast_select_fusion
  236.1 4.4 collective-permute-start
  240.5 45.3 %collective-permute-done = f32[2,512,512]{2,1,0:T(8,128)} collective-permute-done((f32[2,512,512]{2,1,0:T(8,128)}, f32[2,512,512]{2,1,0:T(8,128)}, u32[]{:S(2)}, u32[]{:S(2)}) %collective-permute-start) | collective-permute-done | bytes 2097184 | tf_op jit(solution)/shard_map/ppermute | solution.py:10
  285.9 2.9 select_add_fusion
  289.0 3.4 collective-permute-start.1
  292.5 2.3 collective-permute-done.1
  296.1 90.9 %reduce-scatter.2.cloned.1.call-done = f32[2,16,512]{2,1,0:T(8,128)} async-done(((f32[2,256,512]{2,1,0:T(8,128)}), f32[2,16,512]{2,1,0:T(8,128)}) %reduce-scatter.2.cloned.1.call-update) | async-done | bytes 65552 | tf_op jit(solution)/shard_map/reduce_scatter | solution.py:81
  387.1 1.5 fusion.6
  388.5 97.5 %all-reduce = (f32[]{:T(128)}, f32[]{:T(128)}) all-reduce(f32[]{:T(128)} %get-tuple-element.3, f32[]{:T(128)} %get-tuple-element.2), channel_id=1, replica_groups=mesh['dp'=16,'ctx'=32] {'dp','ctx'}, use_global_device_ids=true, to_apply=%region_2.3 | all-reduce | flops 2 | bytes 16 | tf_op jit(solution)/shard_map/psum | solution.py:95
  487.5 1.5 fusion.4
  (24 shorter events, 7.1 us)
Async XLA Ops:
  9.4 11.8 %copy-start.3 = (bf16[160,2048]{1,0:T(8,128)(2,1)S(1)}, bf16[160,2048]{1,0:T(8,128)(2,1)}, u32[]{:S(2)}) copy-start(bf16[160,2048]{1,0:T(8,128)(2,1)} %param.2) | copy-start | bytes 1966084
  10.6 43.1 %all-to-all-start.3 = ((bf16[32,40,512]{2,1,0:T(8,128)(2,1)}), bf16[32,40,512]{2,1,0:T(8,128)(2,1)S(1)}, u32[]{:S(2)}, u32[]{:S(2)}) async-start(bf16[32,40,512]{2,1,0:T(8,128)(2,1)} %bitcast.9), calls=%async_computation.3 | async-start | bytes 2621440 | tf_op jit(solution)/shard_map/all_to_all | solution.py:76
  21.8 39.0 %copy-start.2 = (bf16[160,2048]{1,0:T(8,128)(2,1)S(1)}, bf16[160,2048]{1,0:T(8,128)(2,1)}, u32[]{:S(2)}) copy-start(bf16[160,2048]{1,0:T(8,128)(2,1)} %param.3) | copy-start | bytes 1966084
  53.7 1.5 copy-start.4
  55.2 38.3 %all-to-all-start.1 = ((bf16[32,40,512]{2,1,0:T(8,128)(2,1)}), bf16[32,40,512]{2,1,0:T(8,128)(2,1)}, u32[]{:S(2)}, u32[]{:S(2)}) async-start(bf16[32,40,512]{2,1,0:T(8,128)(2,1)} %bitcast.3), calls=%async_computation.1 | async-start | bytes 2621440 | tf_op jit(solution)/shard_map/all_to_all | solution.py:74
  95.4 66.4 %all-to-all-start.2 = ((bf16[32,40,1024]{2,1,0:T(8,128)(2,1)}), bf16[32,40,1024]{2,1,0:T(8,128)(2,1)S(1)}, u32[]{:S(2)}, u32[]{:S(2)}) async-start(bf16[32,40,1024]{2,1,0:T(8,128)(2,1)} %bitcast.7), calls=%async_computation.2 | async-start | bytes 5242880 | tf_op jit(solution)/shard_map/all_to_all | solution.py:75
  161.8 2.3 copy-start.1
  164.1 66.4 %all-to-all-start = ((bf16[32,40,1024]{2,1,0:T(8,128)(2,1)}), bf16[32,40,1024]{2,1,0:T(8,128)(2,1)}, u32[]{:S(2)}, u32[]{:S(2)}) async-start(bf16[32,40,1024]{2,1,0:T(8,128)(2,1)} %bitcast.1), calls=%async_computation | async-start | bytes 5242880 | tf_op jit(solution)/shard_map/all_to_all | solution.py:73
  169.6 217.5 %reduce-scatter.2.cloned.1.call-start = ((), (), s32[]{:S(2)}) async-start(), calls=%async_computation.5 | async-start | bytes 1114112 | tf_op jit(solution)/shard_map/reduce_scatter | solution.py:81
  234.2 1.9 copy-start
  236.1 49.8 %collective-permute-start = (f32[2,512,512]{2,1,0:T(8,128)}, f32[2,512,512]{2,1,0:T(8,128)}, u32[]{:S(2)}, u32[]{:S(2)}) collective-permute-start(f32[2,512,512]{2,1,0:T(8,128)} %broadcast_select_fusion), channel_id=1, source_target_pairs={{0,2},{1,3},{2,0},{3,1},{4,6},{5,7},{6,4},{7,5},{8,10},{9,11},{10,... | collective-permute-start | bytes 6291464 | tf_op jit(solution)/shard_map/ppermute | solution.py:10
  289.0 5.7 %collective-permute-start.1 = (f32[2,256,512]{2,1,0:T(8,128)S(1)}, f32[2,256,512]{2,1,0:T(8,128)S(1)}, u32[]{:S(2)}, u32[]{:S(2)}) collective-permute-start(f32[2,256,512]{2,1,0:T(8,128)S(1)} %slice_select_fusion), channel_id=1, source_target_pairs={{0,1},{1,0},{2,3},{3,2},{4,5},{5,4},{6,7},{7,6},{8,9},{9,8},{10,11... | collective-permute-start | bytes 3145736 | tf_op jit(solution)/shard_map/ppermute | solution.py:10
Sparse Core Ops, SparseCore 0:
  296.2 90.8 reduce-scatter.1
where the time goes:
time: 497 us; the launch traced here: 496 us
  waiting for transfers between devices  318 us (64%)
  blocking collectives  97.5 us (20%)
  starting transfers between devices  35 us (7%)
  between operations  15.7 us (3%)
  local copies, waits for them, and re-layouts  12.8 us (3%)
  other arithmetic  9.33 us (2%)
  matrix products  7.31 us (1%)
    psum x1, blocking collectives, on_device(): lax.psum((jnp.sum(act_share * diag_mask), jnp.sum(grad_share * diag_mask)...  97.5 us
    reduce_scatter x1, waiting for transfers between devices, on_device(): shares = lax.psum_scatter(folded, 'dp', scatter_dimension=1, tiled=True)  90.9 us
    all_to_all x1, waiting for transfers between devices, on_device(): lax.all_to_all(grad_rows, 'ctx', split_axis=0, concat_axis=0, tiled=True)  58.3 us
    all_to_all x1, waiting for transfers between devices, on_device(): lax.all_to_all(act_rows, 'ctx', split_axis=0, concat_axis=0, tiled=True)  57.2 us
    ppermute x2, waiting for transfers between devices, swapped(): lax.ppermute(value, axis, [(i, i ^ 1 << apart) for i in range(lax.axis_si...  47.6 us
    all_to_all x1, waiting for transfers between devices, on_device(): lax.all_to_all(act_cols, 'ctx', split_axis=0, concat_axis=0, tiled=True)  32.1 us
    all_to_all x1, waiting for transfers between devices, on_device(): lax.all_to_all(grad_cols, 'ctx', split_axis=0, concat_axis=0, tiled=True)  31.9 us
    all_to_all x1, starting transfers between devices, on_device(): lax.all_to_all(grad_cols, 'ctx', split_axis=0, concat_axis=0, tiled=True)  10.6 us
  transfers between devices with their start and end apart: 7, of which 7 were waited for; matrix products, arithmetic and copies ran while one was open for 2% of the time, Pallas kernels for 0%

commit v1 on v0

v1 whole, which is shorter than its diff:
```python
import jax
import jax.numpy as jnp
from jax import lax
from jax.experimental import pallas as pl
from jax.experimental.pallas import tpu as pltpu
from jax.sharding import PartitionSpec as P

damping = 1.0

NX, NY, NZ = 4, 8, 8
ROWS = 160
HALF = ROWS // 2
W = 2048
HW = W // 2
BLK = 128
NB = HW // BLK
TOKENS = ROWS * 2 * NX * NY * NZ
MESH = pl.DeviceIdType.MESH

STREAMS = ((0, 1, 4), (0, -1, 3), (1, 1, 3), (1, -1, 4))
BASE = (0, 4, 7, 10)
NSLOT = 14


def device(x, y, z, c):
    return (x * (NZ // 2) + z // 2, (z % 2) * (2 * NY) + y * 2 + c)


def kernel(act, grad, act_out, grad_out,
           xb, pk, r1, r2, outbox, inbox, dg, gy, gz, gx, gc,
           loc_sem, raw_s, raw_r, s1_s, s1_r, s2_s, s2_r,
           dg_s, dg_r, out_s, out_r):
    dp = lax.axis_index("dp")
    ctx = lax.axis_index("ctx")
    x = dp // (NZ // 2)
    z = (dp % (NZ // 2)) * 2 + ctx // (2 * NY)
    y = (ctx // 2) % NY
    c = ctx % 2
    par = x % 2

    def at_x(d):
        return device((x + d) % NX, y, z, c)

    def at_y(d):
        return device(x, (y + d) % NY, z, c)

    def at_z(d):
        return device(x, y, (z + d) % NZ, c)

    partner = device(x, y, z, 1 - c)

    def remote(src, dst, ssem, rsem, dev):
        return pltpu.make_async_remote_copy(
            src_ref=src, dst_ref=dst, send_sem=ssem, recv_sem=rsem,
            device_id=dev, device_id_type=MESH)

    barrier = pltpu.get_barrier_semaphore()
    peers = [partner] + [at_x(d) for d in range(1, NX)]
    peers += [at_y(d) for d in range(1, NY)] + [at_z(d) for d in range(1, NZ)]
    for dev in peers:
        pl.semaphore_signal(barrier, inc=1, device_id=dev, device_id_type=MESH)

    own_rows = xb.at[pl.ds(0, ROWS)]

    @pl.when(par == 0)
    def _():
        pltpu.make_async_copy(act, own_rows, loc_sem).start()

    @pl.when(par == 1)
    def _():
        pltpu.make_async_copy(grad, own_rows, loc_sem).start()

    pl.semaphore_wait(barrier, len(peers))

    def raw_copies(own, other):
        copies = []
        for h in range(2):
            cols = pl.ds(h * HW, HW)
            copies.append(remote(
                other.at[pl.ds(0, HALF), cols],
                xb.at[pl.ds(2 * ROWS, HALF), cols],
                raw_s.at[2 * h], raw_r.at[2 * h], at_x(1)))
            copies.append(remote(
                other.at[pl.ds(HALF, HALF), cols],
                xb.at[pl.ds(2 * ROWS + HALF, HALF), cols],
                raw_s.at[2 * h + 1], raw_r.at[2 * h + 1], at_x(-1)))
        copies.append(remote(own, xb.at[pl.ds(ROWS, ROWS)],
                             raw_s.at[4], raw_r.at[4], partner))
        return copies

    @pl.when(par == 0)
    def _():
        for copy in raw_copies(act, grad):
            copy.start()

    @pl.when(par == 1)
    def _():
        for copy in raw_copies(grad, act):
            copy.start()

    raw = raw_copies(act, grad)
    pltpu.make_async_copy(act, own_rows, loc_sem).wait()
    raw[4].wait_recv()

    contract = (((0,), (0,)), ((), ()))

    def gram(row, lo, ro):
        left = xb[pl.ds(row, 2 * ROWS), pl.ds(pl.multiple_of(lo, 256), 256)]
        right = xb[pl.ds(row, 2 * ROWS), pl.ds(pl.multiple_of(ro, 256), 256)]
        return lax.dot_general(left, right, contract,
                               preferred_element_type=jnp.float32)

    upper = (lax.broadcasted_iota(jnp.int32, (256, 256), 0)
             < lax.broadcasted_iota(jnp.int32, (256, 256), 1))

    def store(a, b, value, add):
        for i in range(2):
            for j in range(2):
                part = value[BLK * i:BLK * (i + 1), BLK * j:BLK * (j + 1)]
                if add:
                    part = part + pk[2 * a + i, 2 * b + j]
                pk[2 * a + i, 2 * b + j] = part

    def diagonal_blocks(row, add):
        def step(a, carry):
            first = gram(row, 256 * a, 256 * a)
            second = gram(row, HW + 256 * a, HW + 256 * a)
            store(a, a, jnp.where(upper, first, second), add)
            return carry
        lax.fori_loop(0, 4, step, 0)

    def tile_grid(row, add):
        def step(a, carry):
            for b in range(4):
                low = jnp.where(a > b, HW, 0)
                lo = 256 * a + jnp.where(c == 0, 0, low)
                ro = 256 * b + jnp.where(c == 0, HW, low)
                value = gram(row, lo, ro)

                @pl.when(jnp.logical_or(c == 0, a != b))
                def _():
                    store(a, b, value, add)
            return carry
        lax.fori_loop(0, 4, step, 0)

        @pl.when(c == 1)
        def _():
            diagonal_blocks(row, add)

    tile_grid(0, False)

    relay = []
    for h in range(2):
        for s in range(2):
            raw[2 * h + s].wait_recv()
            rows = pl.ds(2 * ROWS + HALF * s, HALF)
            to = pl.ds(3 * ROWS + HALF * s, HALF)
            cols = pl.ds(h * HW, HW)
            copy = remote(xb.at[rows, cols], xb.at[to, cols],
                          raw_s.at[5 + 2 * h + s], raw_r.at[5 + 2 * h + s], partner)
            copy.start()
            relay.append(copy)
    for copy in relay:
        copy.wait_recv()

    tile_grid(2 * ROWS, True)

    def chunk1(k, o, h):
        if k == 0:
            return pk.at[o, pl.ds(4 * h, 4), pl.ds(0, 64), :]
        return pk.at[pl.ds(4 * h, 4), o, pl.ds(64, 64), :]

    def chunk2(k, o, h):
        if k == 0:
            return pk.at[y, o, pl.ds(32 * h, 32), :]
        return pk.at[o, z, pl.ds(64 + 32 * h, 32), :]

    def ring(chunk, slots, ssem, rsem, axes, between):
        copies = {}
        for t in range(5):
            for i, (h, sign, hops) in enumerate(STREAMS):
                if t > hops:
                    continue
                for k in range(2):
                    pos, at = axes[k]
                    n = NY
                    o = (pos + sign * (hops - t)) % n
                    ref = chunk(k, o, h)
                    if t > 0:
                        copies[k, i, t - 1].wait_recv()
                        ref[...] = ref[...] + slots[k * NSLOT + BASE[i] + t - 1]
                    if t < hops:
                        slot = k * NSLOT + BASE[i] + t
                        copy = remote(ref, slots.at[slot], ssem.at[slot],
                                      rsem.at[slot], at(sign))
                        copy.start()
                        copies[k, i, t] = copy
            between(t)
        return copies

    diag_copies = []

    def diag_send(srcs, dsts, devs, base):
        copies = []
        for n, (src, dst, dev) in enumerate(zip(srcs, dsts, devs)):
            copy = remote(src, dst, dg_s.at[base + n], dg_r.at[base + n], dev)
            copy.start()
            copies.append(copy)
        diag_copies.extend(copies)
        return copies

    pending = {}

    def between1(t):
        if t == 0:
            for i in range(NB):
                cols = pl.ds(pl.multiple_of(c * HW + BLK * i, BLK), BLK)
                part = xb[:, cols].astype(jnp.float32)
                dg[0, pl.ds(i, 1), :] = jnp.sum(part * part, axis=0, keepdims=True)
            pending["y"] = diag_send(
                [dg.at[0]] * 7, [gy.at[d - 1] for d in range(1, NY)],
                [at_y(d) for d in range(1, NY)], 0)
        elif t == 1:
            total = dg[0]
            for d in range(7):
                pending["y"][d].wait_recv()
                total = total + gy[d]
            dg[1] = total
            pending["z"] = diag_send(
                [dg.at[1]] * 7, [gz.at[d - 1] for d in range(1, NZ)],
                [at_z(d) for d in range(1, NZ)], 7)
        elif t == 2:
            total = dg[1]
            for d in range(7):
                pending["z"][d].wait_recv()
                total = total + gz[d]
            gx[x] = total
            pending["x"] = diag_send(
                [gx.at[x]] * 3, [gx.at[x]] * 3,
                [at_x(d) for d in range(1, NX)], 14)
        elif t == 3:
            for d in range(1, NX):
                src = (x - d) % NX
                remote(gx.at[src], gx.at[src], dg_s.at[13 + d], dg_r.at[13 + d],
                       at_x(d)).wait_recv()
            pending["c"] = diag_send([gx], [gc], [partner], 17)
        else:
            pending["c"][0].wait_recv()

    first = ring(chunk1, r1, s1_s, s1_r, ((y, at_y), (z, at_z)), between1)
    second = ring(chunk2, r2, s2_s, s2_r, ((z, at_z), (y, at_y)), lambda t: None)

    piece = pk[y, z]
    flipped = piece.T
    below = (lax.broadcasted_iota(jnp.int32, (BLK, BLK), 0)
             > lax.broadcasted_iota(jnp.int32, (BLK, BLK), 1))
    packed = jnp.logical_and(c == 1, y == z)
    swap = jnp.logical_and(below, packed)
    outbox[0] = jnp.where(swap, flipped, piece)
    outbox[1] = jnp.where(swap, piece, flipped)

    off_a = jnp.where(y > z, NB, 0)
    off_b = jnp.where(y >= z, NB, 0)
    blocks = (
        (y + jnp.where(c == 0, 0, off_a), z + jnp.where(c == 0, NB, off_a)),
        (z + jnp.where(c == 0, NB, off_b), y + jnp.where(c == 0, 0, off_b)),
    )
    me = (dp, ctx)
    sends = []
    for g in range(2):
        bi, bj = blocks[g]
        slot = par * 8 + (x // 2) * 4 + bj % 4
        for s in range(8):
            dev = device(2 * (bi % 2) + s // 4, 2 * (bj // 4) + (bi // 4) % 2,
                         2 * (s % 4) + bi // 8, (bi // 2) % 2)
            is_me = jnp.logical_and(dev[0] == me[0], dev[1] == me[1])
            src = outbox.at[g, pl.ds(16 * s, 16), :]
            dst = inbox.at[slot]
            copy = remote(src, dst, out_s.at[8 * g + s], out_r.at[slot], dev)

            @pl.when(is_me)
            def _():
                pltpu.make_async_copy(src, dst, out_r.at[slot]).start()

            @pl.when(jnp.logical_not(is_me))
            def _():
                copy.start()
            sends.append((copy, is_me))

    mine = [gx[n] for n in range(NX)]
    theirs = [gc[n] for n in range(NX)]
    diag = [(mine[f] + mine[f + 2], theirs[f] + theirs[f + 2]) for f in range(2)]
    row_block = (z % 2) * 8 + (y % 2) * 4 + c * 2 + x // 2
    strip = (x % 2) * 4 + z // 2
    own_half = (row_block // 8) == c
    pick = lax.broadcasted_iota(jnp.int32, (8, BLK), 0) == row_block % 8
    trace = []
    values = []
    for a, b in diag:
        trace.append(jnp.sum(a + b, keepdims=True))
        chosen = jnp.where(own_half, a, b)
        values.append(jnp.sum(jnp.where(pick, chosen, 0.0), axis=0, keepdims=True))
    ratio = jnp.sqrt(trace[0] / trace[1])
    shift = (ratio * damping, damping / ratio)
    scale = 1.0 / TOKENS
    on_diag = (lax.broadcasted_iota(jnp.int32, (16, BLK), 1)
               == lax.broadcasted_iota(jnp.int32, (16, BLK), 0) + 16 * strip)
    for f in range(2):
        out = (act_out, grad_out)[f]
        damped = values[f] * scale + shift[f]
        for j in range(4):
            for n in range(2):
                slot = 8 * f + 4 * n + j
                pltpu.make_async_copy(outbox.at[0, pl.ds(0, 16), :], inbox.at[slot],
                                      out_r.at[slot]).wait()
            here = jnp.logical_and(on_diag, (y // 2) * 4 + j == row_block)
            value = (inbox[8 * f + j] + inbox[8 * f + 4 + j]) * scale
            out[:, BLK * j:BLK * (j + 1)] = jnp.where(here, damped, value)

    for copy, is_me in sends:
        @pl.when(jnp.logical_not(is_me))
        def _():
            copy.wait_send()
    for copy in raw + relay + list(first.values()) + list(second.values()) + diag_copies:
        copy.wait_send()


def on_device(act_input, out_grad):
    f32 = jnp.float32
    piece = jax.ShapeDtypeStruct((16, 4 * BLK), f32)
    any_space = pl.BlockSpec(memory_space=pl.ANY)
    vmem = pl.BlockSpec(memory_space=pltpu.VMEM)
    dma = pltpu.SemaphoreType.DMA
    act_out, grad_out = pl.pallas_call(
        kernel,
        out_shape=(piece, piece),
        in_specs=[any_space, any_space],
        out_specs=(vmem, vmem),
        scratch_shapes=[
            pltpu.VMEM((4 * ROWS, W), jnp.bfloat16),
            pltpu.VMEM((NB, NB, BLK, BLK), f32),
            pltpu.VMEM((2 * NSLOT, 4, 64, BLK), f32),
            pltpu.VMEM((2 * NSLOT, 32, BLK), f32),
            pltpu.VMEM((2, BLK, BLK), f32),
            pltpu.VMEM((16, 16, BLK), f32),
            pltpu.VMEM((2, 8, BLK), f32),
            pltpu.VMEM((7, 8, BLK), f32),
            pltpu.VMEM((7, 8, BLK), f32),
            pltpu.VMEM((NX, 8, BLK), f32),
            pltpu.VMEM((NX, 8, BLK), f32),
            dma,
            dma((9,)), dma((9,)),
            dma((2 * NSLOT,)), dma((2 * NSLOT,)),
            dma((2 * NSLOT,)), dma((2 * NSLOT,)),
            dma((18,)), dma((18,)),
            dma((16,)), dma((16,)),
        ],
        compiler_params=pltpu.CompilerParams(
            collective_id=0, has_side_effects=True,
            vmem_limit_bytes=48 * 1024 * 1024),
        name="kfac",
    )(act_input, out_grad)
    return act_out[None, None], grad_out[None, None]


def solution(mesh):
    placed = (P(("dp", "ctx"), None), P(("dp", "ctx"), None))
    return jax.shard_map(
        on_device,
        mesh=mesh,
        in_specs=placed,
        out_specs=(P("ctx", "dp", None, None), P("ctx", "dp", None, None)),
        check_vma=False,
    )
```

time: 497 us -> 83.5 us (0.17)
  the two profiles are of different devices: /device:TPU:1 before, /device:TPU:57 now
where the time goes in v1:
time: 83.5 us; the launch traced here: 83.3 us
  Pallas kernels  79.3 us (95%)
  local copies, waits for them, and re-layouts  3.4 us (4%)
    pallas_call x1, Pallas kernels, on_device(): pl.pallas_call(kernel, out_shape=(piece, piece), in_specs=[any_space, any...  79.3 us
    unnamed x6, local copies, waits for them, and re-layouts  3.4 us

profile of v1, /device:TPU:57, one launch (start us, length us, event | category | flops | bytes accessed | tf_op | source)
XLA Modules:
  0.0 83.3 jit_solution(5897880502248398521)
XLA Ops:
  0.6 0.0 copy-start
  0.6 1.1 %copy-done = bf16[160,2048]{1,0:T(8,128)(2,1)S(1)} copy-done((bf16[160,2048]{1,0:T(8,128)(2,1)S(1)}, bf16[160,2048]{1,0:T(8,128)(2,1)}, u32[]{:S(2)}) %copy-start) | copy-done | bytes 655384
  1.7 0.0 copy-start.1
  1.7 1.1 %copy-done.1 = bf16[160,2048]{1,0:T(8,128)(2,1)S(1)} copy-done((bf16[160,2048]{1,0:T(8,128)(2,1)S(1)}, bf16[160,2048]{1,0:T(8,128)(2,1)}, u32[]{:S(2)}) %copy-start.1) | copy-done | bytes 655384
  2.8 79.3 %kfac.1 = (f32[16,512]{1,0:T(8,128)S(1)}, f32[16,512]{1,0:T(8,128)S(1)}) custom-call(bf16[160,2048]{1,0:T(8,128)(2,1)S(1)} %copy-done, bf16[160,2048]{1,0:T(8,128)(2,1)S(1)} %copy-done.1), custom_call_target="tpu_custom_call" | custom-call | tf_op jit(solution)/shard_map/kfac/pallas_call | solution.py:334
  82.1 0.6 copy.6
  82.7 0.6 copy.7
Async XLA Ops:
  0.6 1.1 %copy-start = (bf16[160,2048]{1,0:T(8,128)(2,1)S(1)}, bf16[160,2048]{1,0:T(8,128)(2,1)}, u32[]{:S(2)}) copy-start(bf16[160,2048]{1,0:T(8,128)(2,1)} %act.1) | copy-start | bytes 1966084
  1.7 1.1 %copy-start.1 = (bf16[160,2048]{1,0:T(8,128)(2,1)S(1)}, bf16[160,2048]{1,0:T(8,128)(2,1)}, u32[]{:S(2)}) copy-start(bf16[160,2048]{1,0:T(8,128)(2,1)} %grad.1) | copy-start | bytes 1966084

commit v2 on v1

--- a/solution.py
+++ b/solution.py
@@ -104,10 +104,8 @@
 
     contract = (((0,), (0,)), ((), ()))
 
-    def gram(row, lo, ro):
-        left = xb[pl.ds(row, 2 * ROWS), pl.ds(pl.multiple_of(lo, 256), 256)]
-        right = xb[pl.ds(row, 2 * ROWS), pl.ds(pl.multiple_of(ro, 256), 256)]
-        return lax.dot_general(left, right, contract,
+    def product(rows, left, right):
+        return lax.dot_general(xb[rows, left], xb[rows, right], contract,
                                preferred_element_type=jnp.float32)
 
     upper = (lax.broadcasted_iota(jnp.int32, (256, 256), 0)
@@ -121,31 +119,30 @@
                     part = part + pk[2 * a + i, 2 * b + j]
                 pk[2 * a + i, 2 * b + j] = part
 
-    def diagonal_blocks(row, add):
-        def step(a, carry):
-            first = gram(row, 256 * a, 256 * a)
-            second = gram(row, HW + 256 * a, HW + 256 * a)
-            store(a, a, jnp.where(upper, first, second), add)
-            return carry
-        lax.fori_loop(0, 4, step, 0)
-
     def tile_grid(row, add):
-        def step(a, carry):
-            for b in range(4):
-                low = jnp.where(a > b, HW, 0)
-                lo = 256 * a + jnp.where(c == 0, 0, low)
-                ro = 256 * b + jnp.where(c == 0, HW, low)
-                value = gram(row, lo, ro)
-
-                @pl.when(jnp.logical_or(c == 0, a != b))
-                def _():
-                    store(a, b, value, add)
-            return carry
-        lax.fori_loop(0, 4, step, 0)
+        rows = pl.ds(row, 2 * ROWS)
+
+        @pl.when(c == 0)
+        def _():
+            for a in range(4):
+                value = product(rows, pl.ds(256 * a, 256), pl.ds(HW, HW))
+                for b in range(4):
+                    store(a, b, value[:, 256 * b:256 * (b + 1)], add)
 
         @pl.when(c == 1)
         def _():
-            diagonal_blocks(row, add)
+            for a in range(4):
+                first = product(rows, pl.ds(256 * a, 256), pl.ds(256 * a, HW - 256 * a))
+                second = product(rows, pl.ds(HW + 256 * a, 256), pl.ds(HW, 256 * (a + 1)))
+                for b in range(4):
+                    high = first[:, 256 * (b - a):256 * (b - a + 1)] if b >= a else None
+                    low = second[:, 256 * b:256 * (b + 1)] if b <= a else None
+                    if high is None:
+                        store(a, b, low, add)
+                    elif low is None:
+                        store(a, b, high, add)
+                    else:
+                        store(a, b, jnp.where(upper, high, low), add)
 
     tile_grid(0, False)
 
@@ -169,11 +166,6 @@
         if k == 0:
             return pk.at[o, pl.ds(4 * h, 4), pl.ds(0, 64), :]
         return pk.at[pl.ds(4 * h, 4), o, pl.ds(64, 64), :]
-
-    def chunk2(k, o, h):
-        if k == 0:
-            return pk.at[y, o, pl.ds(32 * h, 32), :]
-        return pk.at[o, z, pl.ds(64 + 32 * h, 32), :]
 
     def ring(chunk, slots, ssem, rsem, axes, between):
         copies = {}
@@ -248,9 +240,23 @@
             pending["c"][0].wait_recv()
 
     first = ring(chunk1, r1, s1_s, s1_r, ((y, at_y), (z, at_z)), between1)
-    second = ring(chunk2, r2, s2_s, s2_r, ((z, at_z), (y, at_y)), lambda t: None)
-
-    piece = pk[y, z]
+    second = []
+    for d in (4, 3, 5, 2, 6, 1, 7):
+        for k in range(2):
+            if k == 0:
+                src, dev = pk.at[y, (z + d) % NZ, pl.ds(0, 64), :], at_z(d)
+            else:
+                src, dev = pk.at[(y + d) % NY, z, pl.ds(64, 64), :], at_y(d)
+            slot = 7 * k + d - 1
+            copy = remote(src, r2.at[slot], s2_s.at[slot], s2_r.at[slot], dev)
+            copy.start()
+            second.append((k, slot, copy))
+    sums = [pk[y, z, pl.ds(0, 64), :], pk[y, z, pl.ds(64, 64), :]]
+    for k, slot, copy in sorted(second, key=lambda e: min(e[1] % 7, 6 - e[1] % 7)):
+        copy.wait_recv()
+        sums[k] = sums[k] + r2[slot]
+
+    piece = jnp.concatenate(sums, axis=0)
     flipped = piece.T
     below = (lax.broadcasted_iota(jnp.int32, (BLK, BLK), 0)
              > lax.broadcasted_iota(jnp.int32, (BLK, BLK), 1))
@@ -321,14 +327,14 @@
         @pl.when(jnp.logical_not(is_me))
         def _():
             copy.wait_send()
-    for copy in raw + relay + list(first.values()) + list(second.values()) + diag_copies:
+    for copy in raw + relay + list(first.values()) + [copy for _, _, copy in second] + diag_copies:
         copy.wait_send()
 
 
 def on_device(act_input, out_grad):
     f32 = jnp.float32
     piece = jax.ShapeDtypeStruct((16, 4 * BLK), f32)
-    any_space = pl.BlockSpec(memory_space=pl.ANY)
+    any_space = pl.BlockSpec(memory_space=pltpu.HBM)
     vmem = pl.BlockSpec(memory_space=pltpu.VMEM)
     dma = pltpu.SemaphoreType.DMA
     act_out, grad_out = pl.pallas_call(
@@ -340,7 +346,7 @@
             pltpu.VMEM((4 * ROWS, W), jnp.bfloat16),
             pltpu.VMEM((NB, NB, BLK, BLK), f32),
             pltpu.VMEM((2 * NSLOT, 4, 64, BLK), f32),
-            pltpu.VMEM((2 * NSLOT, 32, BLK), f32),
+            pltpu.VMEM((14, 64, BLK), f32),
             pltpu.VMEM((2, BLK, BLK), f32),
             pltpu.VMEM((16, 16, BLK), f32),
             pltpu.VMEM((2, 8, BLK), f32),
@@ -357,7 +363,7 @@
         ],
         compiler_params=pltpu.CompilerParams(
             collective_id=0, has_side_effects=True,
-            vmem_limit_bytes=48 * 1024 * 1024),
+            vmem_limit_bytes=62 * 1024 * 1024),
         name="kfac",
     )(act_input, out_grad)
     return act_out[None, None], grad_out[None, None]

time: 83.5 us -> 73.3 us (0.88)
  the two profiles are of different devices: /device:TPU:57 before, /device:TPU:31 now
where the time goes in v2:
time: 73.3 us; the launch traced here: 73.1 us
  Pallas kernels  70.4 us (96%)
  local copies, waits for them, and re-layouts  2 us (3%)
    pallas_call x1, Pallas kernels, on_device(): pl.pallas_call(kernel, out_shape=(piece, piece), in_specs=[any_space, any...  70.4 us
    unnamed x4, local copies, waits for them, and re-layouts  2 us

profile of v2, /device:TPU:31, one launch (start us, length us, event | category | flops | bytes accessed | tf_op | source)
XLA Modules:
  0.0 73.1 jit_solution(4054444458219962433)
XLA Ops:
  0.6 70.4 %kfac.1 = (f32[16,512]{1,0:T(8,128)}, f32[16,512]{1,0:T(8,128)}) custom-call(bf16[160,2048]{1,0:T(8,128)(2,1)} %act.1, bf16[160,2048]{1,0:T(8,128)(2,1)} %grad.1), custom_call_target="tpu_custom_call" | custom-call | tf_op jit(solution)/shard_map/kfac/pallas_call | solution.py:340
  71.1 0.0 copy-start
  71.1 1.4 %copy.6 = f32[1,1,16,512]{3,2,1,0:T(8,128)} copy(f32[1,1,16,512]{3,2,1,0:T(8,128)} %bitcast.3) | data formatting | bytes 65536
  72.5 0.0 copy-done
  72.5 0.6 copy.7
Async XLA Ops:
  71.1 1.4 %copy-start = (f32[16,512]{1,0:T(8,128)S(1)}, f32[16,512]{1,0:T(8,128)}, u32[]{:S(2)}) copy-start(f32[16,512]{1,0:T(8,128)} %get-tuple-element.5) | copy-start | bytes 98308

commit v3 on v2

--- a/solution.py
+++ b/solution.py
@@ -20,6 +20,8 @@
 STREAMS = ((0, 1, 4), (0, -1, 3), (1, 1, 3), (1, -1, 4))
 BASE = (0, 4, 7, 10)
 NSLOT = 14
+CHUNK = 256
+CODE_TOP = 2.0 ** 15
 
 
 def device(x, y, z, c):
@@ -27,7 +29,7 @@
 
 
 def kernel(act, grad, act_out, grad_out,
-           xb, pk, r1, r2, outbox, inbox, dg, gy, gz, gx, gc,
+           xb, pk, q1, r1, r2, outbox, inbox, dg, gy, gz, gx, gc,
            loc_sem, raw_s, raw_r, s1_s, s1_r, s2_s, s2_r,
            dg_s, dg_r, out_s, out_r):
     dp = lax.axis_index("dp")
@@ -167,7 +169,25 @@
             return pk.at[o, pl.ds(4 * h, 4), pl.ds(0, 64), :]
         return pk.at[pl.ds(4 * h, 4), o, pl.ds(64, 64), :]
 
-    def ring(chunk, slots, ssem, rsem, axes, between):
+    def encode(value, ref):
+        n = value.shape[0]
+        tiles = value.reshape(n // 8, 8, BLK)
+        top = jnp.max(jnp.abs(tiles), axis=0)
+        scale = (CODE_TOP / jnp.maximum(top, 1e-30)).astype(jnp.bfloat16)
+        v = tiles * scale.astype(jnp.float32)[None]
+        for _ in range(3):
+            v = v * jnp.abs(v)
+        ref[pl.ds(0, n), :] = v.reshape(n, BLK).astype(jnp.bfloat16)
+        ref[pl.ds(n, 16), :] = jnp.concatenate([scale, scale], axis=0)
+
+    def decode(ref, n):
+        y = ref[pl.ds(0, n), :].astype(jnp.float32).reshape(n // 8, 8, BLK)
+        inverse = 1.0 / ref[pl.ds(n, 16), :].astype(jnp.float32)[0:8]
+        root = lax.rsqrt(lax.rsqrt(jnp.maximum(jnp.abs(y), 1.2e-38)))
+        root = root * lax.rsqrt(root)
+        return (jnp.where(y < 0, -root, root) * inverse[None]).reshape(n, BLK)
+
+    def ring(chunk, sent, slots, ssem, rsem, axes, between):
         copies = {}
         for t in range(5):
             for i, (h, sign, hops) in enumerate(STREAMS):
@@ -175,15 +195,18 @@
                     continue
                 for k in range(2):
                     pos, at = axes[k]
-                    n = NY
-                    o = (pos + sign * (hops - t)) % n
+                    o = (pos + sign * (hops - t)) % NY
                     ref = chunk(k, o, h)
+                    value = ref[...].reshape(CHUNK, BLK)
                     if t > 0:
                         copies[k, i, t - 1].wait_recv()
-                        ref[...] = ref[...] + slots[k * NSLOT + BASE[i] + t - 1]
-                    if t < hops:
+                        value = value + decode(slots.at[k * NSLOT + BASE[i] + t - 1], CHUNK)
+                    if t == hops:
+                        ref[...] = value.reshape(4, 64, BLK)
+                    else:
                         slot = k * NSLOT + BASE[i] + t
-                        copy = remote(ref, slots.at[slot], ssem.at[slot],
+                        encode(value, sent.at[slot])
+                        copy = remote(sent.at[slot], slots.at[slot], ssem.at[slot],
                                       rsem.at[slot], at(sign))
                         copy.start()
                         copies[k, i, t] = copy
@@ -239,7 +262,7 @@
         else:
             pending["c"][0].wait_recv()
 
-    first = ring(chunk1, r1, s1_s, s1_r, ((y, at_y), (z, at_z)), between1)
+    first = ring(chunk1, q1, r1, s1_s, s1_r, ((y, at_y), (z, at_z)), between1)
     second = []
     for d in (4, 3, 5, 2, 6, 1, 7):
         for k in range(2):
@@ -345,7 +368,8 @@
         scratch_shapes=[
             pltpu.VMEM((4 * ROWS, W), jnp.bfloat16),
             pltpu.VMEM((NB, NB, BLK, BLK), f32),
-            pltpu.VMEM((2 * NSLOT, 4, 64, BLK), f32),
+            pltpu.VMEM((2 * NSLOT, CHUNK + 16, BLK), jnp.bfloat16),
+            pltpu.VMEM((2 * NSLOT, CHUNK + 16, BLK), jnp.bfloat16),
             pltpu.VMEM((14, 64, BLK), f32),
             pltpu.VMEM((2, BLK, BLK), f32),
             pltpu.VMEM((16, 16, BLK), f32),

time: 73.3 us -> 66.5 us (0.907)
  Pallas kernels: 70.4 us -> 63.7 us
    pallas_call x1, Pallas kernels: 70.4 us -> 63.7 us  [on_device(): pl.pallas_call(kernel, out_shape=(piece, piece), in_specs=[any_space, any...]
where the time goes in v3:
time: 66.5 us; the launch traced here: 66.3 us
  Pallas kernels  63.7 us (96%)
  local copies, waits for them, and re-layouts  2 us (3%)
    pallas_call x1, Pallas kernels, on_device(): pl.pallas_call(kernel, out_shape=(piece, piece), in_specs=[any_space, any...  63.7 us
    unnamed x4, local copies, waits for them, and re-layouts  2 us

profile of v3, /device:TPU:31, one launch (start us, length us, event | category | flops | bytes accessed | tf_op | source)
XLA Modules:
  0.0 66.3 jit_solution(14815459158510974220)
XLA Ops:
  0.6 63.7 %kfac.1 = (f32[16,512]{1,0:T(8,128)}, f32[16,512]{1,0:T(8,128)}) custom-call(bf16[160,2048]{1,0:T(8,128)(2,1)} %act.1, bf16[160,2048]{1,0:T(8,128)(2,1)} %grad.1), custom_call_target="tpu_custom_call" | custom-call | tf_op jit(solution)/shard_map/kfac/pallas_call | solution.py:363
  64.3 0.0 copy-start
  64.3 1.4 %copy.6 = f32[1,1,16,512]{3,2,1,0:T(8,128)} copy(f32[1,1,16,512]{3,2,1,0:T(8,128)} %bitcast.3) | data formatting | bytes 65536
  65.7 0.0 copy-done
  65.7 0.6 copy.7
Async XLA Ops:
  64.3 1.4 %copy-start = (f32[16,512]{1,0:T(8,128)S(1)}, f32[16,512]{1,0:T(8,128)}, u32[]{:S(2)}) copy-start(f32[16,512]{1,0:T(8,128)} %get-tuple-element.5) | copy-start | bytes 98308

commit v4 on v3

--- a/solution.py
+++ b/solution.py
@@ -17,10 +17,12 @@
 TOKENS = ROWS * 2 * NX * NY * NZ
 MESH = pl.DeviceIdType.MESH
 
-STREAMS = ((0, 1, 4), (0, -1, 3), (1, 1, 3), (1, -1, 4))
-BASE = (0, 4, 7, 10)
-NSLOT = 14
-CHUNK = 256
+STREAMS = ((0, 1, 4), (1, -1, 4), (2, 1, 4), (3, -1, 4),
+           (1, 1, 3), (0, -1, 3), (3, 1, 3), (2, -1, 3))
+BASE = (0, 4, 8, 12, 16, 19, 22, 25)
+NSLOT = 28
+RAW = 2
+CHUNK = 128
 CODE_TOP = 2.0 ** 15
 
 
@@ -29,7 +31,7 @@
 
 
 def kernel(act, grad, act_out, grad_out,
-           xb, pk, q1, r1, r2, outbox, inbox, dg, gy, gz, gx, gc,
+           xb, pk, q1, r1, q2, r2, outbox, inbox, dg, gy, gz, gx, gc,
            loc_sem, raw_s, raw_r, s1_s, s1_r, s2_s, s2_r,
            dg_s, dg_r, out_s, out_r):
     dp = lax.axis_index("dp")
@@ -76,8 +78,8 @@
 
     def raw_copies(own, other):
         copies = []
-        for h in range(2):
-            cols = pl.ds(h * HW, HW)
+        for h in range(RAW):
+            cols = pl.ds(h * (W // RAW), W // RAW)
             copies.append(remote(
                 other.at[pl.ds(0, HALF), cols],
                 xb.at[pl.ds(2 * ROWS, HALF), cols],
@@ -87,7 +89,7 @@
                 xb.at[pl.ds(2 * ROWS + HALF, HALF), cols],
                 raw_s.at[2 * h + 1], raw_r.at[2 * h + 1], at_x(-1)))
         copies.append(remote(own, xb.at[pl.ds(ROWS, ROWS)],
-                             raw_s.at[4], raw_r.at[4], partner))
+                             raw_s.at[2 * RAW], raw_r.at[2 * RAW], partner))
         return copies
 
     @pl.when(par == 0)
@@ -102,7 +104,7 @@
 
     raw = raw_copies(act, grad)
     pltpu.make_async_copy(act, own_rows, loc_sem).wait()
-    raw[4].wait_recv()
+    raw[2 * RAW].wait_recv()
 
     contract = (((0,), (0,)), ((), ()))
 
@@ -149,14 +151,15 @@
     tile_grid(0, False)
 
     relay = []
-    for h in range(2):
+    for h in range(RAW):
         for s in range(2):
             raw[2 * h + s].wait_recv()
             rows = pl.ds(2 * ROWS + HALF * s, HALF)
             to = pl.ds(3 * ROWS + HALF * s, HALF)
-            cols = pl.ds(h * HW, HW)
+            cols = pl.ds(h * (W // RAW), W // RAW)
+            slot = 2 * RAW + 1 + 2 * h + s
             copy = remote(xb.at[rows, cols], xb.at[to, cols],
-                          raw_s.at[5 + 2 * h + s], raw_r.at[5 + 2 * h + s], partner)
+                          raw_s.at[slot], raw_r.at[slot], partner)
             copy.start()
             relay.append(copy)
     for copy in relay:
@@ -166,8 +169,8 @@
 
     def chunk1(k, o, h):
         if k == 0:
-            return pk.at[o, pl.ds(4 * h, 4), pl.ds(0, 64), :]
-        return pk.at[pl.ds(4 * h, 4), o, pl.ds(64, 64), :]
+            return pk.at[o, pl.ds(2 * h, 2), pl.ds(0, 64), :]
+        return pk.at[pl.ds(2 * h, 2), o, pl.ds(64, 64), :]
 
     def encode(value, ref):
         n = value.shape[0]
@@ -202,7 +205,7 @@
                         copies[k, i, t - 1].wait_recv()
                         value = value + decode(slots.at[k * NSLOT + BASE[i] + t - 1], CHUNK)
                     if t == hops:
-                        ref[...] = value.reshape(4, 64, BLK)
+                        ref[...] = value.reshape(2, 64, BLK)
                     else:
                         slot = k * NSLOT + BASE[i] + t
                         encode(value, sent.at[slot])
@@ -235,7 +238,7 @@
             pending["y"] = diag_send(
                 [dg.at[0]] * 7, [gy.at[d - 1] for d in range(1, NY)],
                 [at_y(d) for d in range(1, NY)], 0)
-        elif t == 1:
+        elif t == 2:
             total = dg[0]
             for d in range(7):
                 pending["y"][d].wait_recv()
@@ -244,40 +247,42 @@
             pending["z"] = diag_send(
                 [dg.at[1]] * 7, [gz.at[d - 1] for d in range(1, NZ)],
                 [at_z(d) for d in range(1, NZ)], 7)
-        elif t == 2:
-            total = dg[1]
-            for d in range(7):
-                pending["z"][d].wait_recv()
-                total = total + gz[d]
-            gx[x] = total
-            pending["x"] = diag_send(
-                [gx.at[x]] * 3, [gx.at[x]] * 3,
-                [at_x(d) for d in range(1, NX)], 14)
-        elif t == 3:
-            for d in range(1, NX):
-                src = (x - d) % NX
-                remote(gx.at[src], gx.at[src], dg_s.at[13 + d], dg_r.at[13 + d],
-                       at_x(d)).wait_recv()
-            pending["c"] = diag_send([gx], [gc], [partner], 17)
-        else:
-            pending["c"][0].wait_recv()
+
+    def diag_finish():
+        total = dg[1]
+        for d in range(7):
+            pending["z"][d].wait_recv()
+            total = total + gz[d]
+        gx[x] = total
+        diag_send([gx.at[x]] * 3, [gx.at[x]] * 3, [at_x(d) for d in range(1, NX)], 14)
+
+    def diag_share():
+        for d in range(1, NX):
+            src = (x - d) % NX
+            remote(gx.at[src], gx.at[src], dg_s.at[13 + d], dg_r.at[13 + d],
+                   at_x(d)).wait_recv()
+        return diag_send([gx], [gc], [partner], 17)[0]
 
     first = ring(chunk1, q1, r1, s1_s, s1_r, ((y, at_y), (z, at_z)), between1)
     second = []
     for d in (4, 3, 5, 2, 6, 1, 7):
         for k in range(2):
             if k == 0:
-                src, dev = pk.at[y, (z + d) % NZ, pl.ds(0, 64), :], at_z(d)
+                value, dev = pk[y, (z + d) % NZ, pl.ds(0, 64), :], at_z(d)
             else:
-                src, dev = pk.at[(y + d) % NY, z, pl.ds(64, 64), :], at_y(d)
+                value, dev = pk[(y + d) % NY, z, pl.ds(64, 64), :], at_y(d)
             slot = 7 * k + d - 1
-            copy = remote(src, r2.at[slot], s2_s.at[slot], s2_r.at[slot], dev)
+            encode(value, q2.at[slot])
+            copy = remote(q2.at[slot], r2.at[slot], s2_s.at[slot], s2_r.at[slot], dev)
             copy.start()
             second.append((k, slot, copy))
+    diag_finish()
+    shared = diag_share()
     sums = [pk[y, z, pl.ds(0, 64), :], pk[y, z, pl.ds(64, 64), :]]
     for k, slot, copy in sorted(second, key=lambda e: min(e[1] % 7, 6 - e[1] % 7)):
         copy.wait_recv()
-        sums[k] = sums[k] + r2[slot]
+        sums[k] = sums[k] + decode(r2.at[slot], 64)
+    shared.wait_recv()
 
     piece = jnp.concatenate(sums, axis=0)
     flipped = piece.T
@@ -370,7 +375,8 @@
             pltpu.VMEM((NB, NB, BLK, BLK), f32),
             pltpu.VMEM((2 * NSLOT, CHUNK + 16, BLK), jnp.bfloat16),
             pltpu.VMEM((2 * NSLOT, CHUNK + 16, BLK), jnp.bfloat16),
-            pltpu.VMEM((14, 64, BLK), f32),
+            pltpu.VMEM((14, 80, BLK), jnp.bfloat16),
+            pltpu.VMEM((14, 80, BLK), jnp.bfloat16),
             pltpu.VMEM((2, BLK, BLK), f32),
             pltpu.VMEM((16, 16, BLK), f32),
             pltpu.VMEM((2, 8, BLK), f32),
@@ -379,7 +385,7 @@
             pltpu.VMEM((NX, 8, BLK), f32),
             pltpu.VMEM((NX, 8, BLK), f32),
             dma,
-            dma((9,)), dma((9,)),
+            dma((4 * RAW + 1,)), dma((4 * RAW + 1,)),
             dma((2 * NSLOT,)), dma((2 * NSLOT,)),
             dma((2 * NSLOT,)), dma((2 * NSLOT,)),
             dma((18,)), dma((18,)),

time: 66.5 us -> 63.2 us (0.950)
  Pallas kernels: 63.7 us -> 60.4 us
    pallas_call x1, Pallas kernels: 63.7 us -> 60.4 us  [on_device(): pl.pallas_call(kernel, out_shape=(piece, piece), in_specs=[any_space, any...]
where the time goes in v4:
time: 63.2 us; the launch traced here: 63 us
  Pallas kernels  60.4 us (96%)
  local copies, waits for them, and re-layouts  2 us (3%)
  between operations  0.65 us (1%)
    pallas_call x1, Pallas kernels, on_device(): pl.pallas_call(kernel, out_shape=(piece, piece), in_specs=[any_space, any...  60.4 us
    unnamed x4, local copies, waits for them, and re-layouts  2 us

profile of v4, /device:TPU:31, one launch (start us, length us, event | category | flops | bytes accessed | tf_op | source)
XLA Modules:
  0.0 63.0 jit_solution(12528504512781638182)
XLA Ops:
  0.6 60.4 %kfac.1 = (f32[16,512]{1,0:T(8,128)}, f32[16,512]{1,0:T(8,128)}) custom-call(bf16[160,2048]{1,0:T(8,128)(2,1)} %act.1, bf16[160,2048]{1,0:T(8,128)(2,1)} %grad.1), custom_call_target="tpu_custom_call" | custom-call | tf_op jit(solution)/shard_map/kfac/pallas_call | solution.py:368
  61.0 0.0 copy-start
  61.0 1.4 %copy.6 = f32[1,1,16,512]{3,2,1,0:T(8,128)} copy(f32[1,1,16,512]{3,2,1,0:T(8,128)} %bitcast.3) | data formatting | bytes 65536
  62.4 0.0 copy-done
  62.4 0.6 copy.7
Async XLA Ops:
  61.0 1.4 %copy-start = (f32[16,512]{1,0:T(8,128)S(1)}, f32[16,512]{1,0:T(8,128)}, u32[]{:S(2)}) copy-start(f32[16,512]{1,0:T(8,128)} %get-tuple-element.5) | copy-start | bytes 98308

commit v5 on v4

--- a/solution.py
+++ b/solution.py
@@ -31,7 +31,7 @@
 
 
 def kernel(act, grad, act_out, grad_out,
-           xb, pk, q1, r1, q2, r2, outbox, inbox, dg, gy, gz, gx, gc,
+           xb, ob, pk, q1, r1, q2, r2, outbox, inbox, dl, dg, gd, gy, gz, gx, gc,
            loc_sem, raw_s, raw_r, s1_s, s1_r, s2_s, s2_r,
            dg_s, dg_r, out_s, out_r):
     dp = lax.axis_index("dp")
@@ -68,11 +68,13 @@
 
     @pl.when(par == 0)
     def _():
-        pltpu.make_async_copy(act, own_rows, loc_sem).start()
+        pltpu.make_async_copy(act, own_rows, loc_sem.at[0]).start()
+        pltpu.make_async_copy(grad, ob, loc_sem.at[1]).start()
 
     @pl.when(par == 1)
     def _():
-        pltpu.make_async_copy(grad, own_rows, loc_sem).start()
+        pltpu.make_async_copy(grad, own_rows, loc_sem.at[0]).start()
+        pltpu.make_async_copy(act, ob, loc_sem.at[1]).start()
 
     pl.semaphore_wait(barrier, len(peers))
 
@@ -103,7 +105,32 @@
             copy.start()
 
     raw = raw_copies(act, grad)
-    pltpu.make_async_copy(act, own_rows, loc_sem).wait()
+    pltpu.make_async_copy(act, own_rows, loc_sem.at[0]).wait()
+    pltpu.make_async_copy(act, ob, loc_sem.at[1]).wait()
+
+    diag_copies = []
+
+    def diag_send(srcs, dsts, devs, base):
+        copies = []
+        for n, (src, dst, dev) in enumerate(zip(srcs, dsts, devs)):
+            copy = remote(src, dst, dg_s.at[base + n], dg_r.at[base + n], dev)
+            copy.start()
+            copies.append(copy)
+        diag_copies.extend(copies)
+        return copies
+
+    def diag_sum(first, copies, slots, to):
+        total = dg[first]
+        for n, copy in enumerate(copies):
+            copy.wait_recv()
+            total = total + slots[n]
+        dg[to] = total
+
+    for tokens, f in ((own_rows, par), (ob, 1 - par)):
+        for i in range(2 * NB):
+            part = tokens[:, BLK * i:BLK * (i + 1)].astype(jnp.float32)
+            dl[i // NB, f, pl.ds(i % NB, 1), :] = jnp.sum(part * part, axis=0, keepdims=True)
+    pending = {"d": diag_send([dl.at[1 - c]], [gd.at[0]], [partner], 0)}
     raw[2 * RAW].wait_recv()
 
     contract = (((0,), (0,)), ((), ()))
@@ -150,6 +177,11 @@
 
     tile_grid(0, False)
 
+    dg[0] = dl[c]
+    diag_sum(0, pending["d"], gd, 0)
+    pending["y"] = diag_send([dg.at[0]] * 7, [gy.at[d - 1] for d in range(1, NY)],
+                             [at_y(d) for d in range(1, NY)], 1)
+
     relay = []
     for h in range(RAW):
         for s in range(2):
@@ -162,6 +194,9 @@
                           raw_s.at[slot], raw_r.at[slot], partner)
             copy.start()
             relay.append(copy)
+    diag_sum(0, pending["y"], gy, 1)
+    pending["z"] = diag_send([dg.at[1]] * 7, [gz.at[d - 1] for d in range(1, NZ)],
+                             [at_z(d) for d in range(1, NZ)], 8)
     for copy in relay:
         copy.wait_recv()
 
@@ -171,24 +206,30 @@
         if k == 0:
             return pk.at[o, pl.ds(2 * h, 2), pl.ds(0, 64), :]
         return pk.at[pl.ds(2 * h, 2), o, pl.ds(64, 64), :]
+
+    def power(v):
+        for _ in range(3):
+            v = v * jnp.abs(v)
+        return v
+
+    def root(y):
+        r = lax.rsqrt(lax.rsqrt(jnp.maximum(jnp.abs(y), 1.2e-38)))
+        r = r * lax.rsqrt(r)
+        return jnp.where(y < 0, -r, r)
 
     def encode(value, ref):
         n = value.shape[0]
         tiles = value.reshape(n // 8, 8, BLK)
         top = jnp.max(jnp.abs(tiles), axis=0)
         scale = (CODE_TOP / jnp.maximum(top, 1e-30)).astype(jnp.bfloat16)
-        v = tiles * scale.astype(jnp.float32)[None]
-        for _ in range(3):
-            v = v * jnp.abs(v)
-        ref[pl.ds(0, n), :] = v.reshape(n, BLK).astype(jnp.bfloat16)
+        y = power(tiles * scale.astype(jnp.float32)[None])
+        ref[pl.ds(0, n), :] = y.reshape(n, BLK).astype(jnp.bfloat16)
         ref[pl.ds(n, 16), :] = jnp.concatenate([scale, scale], axis=0)
 
     def decode(ref, n):
         y = ref[pl.ds(0, n), :].astype(jnp.float32).reshape(n // 8, 8, BLK)
         inverse = 1.0 / ref[pl.ds(n, 16), :].astype(jnp.float32)[0:8]
-        root = lax.rsqrt(lax.rsqrt(jnp.maximum(jnp.abs(y), 1.2e-38)))
-        root = root * lax.rsqrt(root)
-        return (jnp.where(y < 0, -root, root) * inverse[None]).reshape(n, BLK)
+        return (root(y) * inverse[None]).reshape(n, BLK)
 
     def ring(chunk, sent, slots, ssem, rsem, axes, between):
         copies = {}
@@ -216,54 +257,34 @@
             between(t)
         return copies
 
-    diag_copies = []
-
-    def diag_send(srcs, dsts, devs, base):
-        copies = []
-        for n, (src, dst, dev) in enumerate(zip(srcs, dsts, devs)):
-            copy = remote(src, dst, dg_s.at[base + n], dg_r.at[base + n], dev)
-            copy.start()
-            copies.append(copy)
-        diag_copies.extend(copies)
-        return copies
-
-    pending = {}
-
     def between1(t):
-        if t == 0:
-            for i in range(NB):
-                cols = pl.ds(pl.multiple_of(c * HW + BLK * i, BLK), BLK)
-                part = xb[:, cols].astype(jnp.float32)
-                dg[0, pl.ds(i, 1), :] = jnp.sum(part * part, axis=0, keepdims=True)
-            pending["y"] = diag_send(
-                [dg.at[0]] * 7, [gy.at[d - 1] for d in range(1, NY)],
-                [at_y(d) for d in range(1, NY)], 0)
+        if t == 1:
+            diag_sum(1, pending["z"], gz, 2)
+            pending["x"] = diag_send([dg.at[2]] * 3, [gx.at[d - 1] for d in range(1, NX)],
+                                     [at_x(d) for d in range(1, NX)], 15)
         elif t == 2:
-            total = dg[0]
-            for d in range(7):
-                pending["y"][d].wait_recv()
-                total = total + gy[d]
-            dg[1] = total
-            pending["z"] = diag_send(
-                [dg.at[1]] * 7, [gz.at[d - 1] for d in range(1, NZ)],
-                [at_z(d) for d in range(1, NZ)], 7)
-
-    def diag_finish():
-        total = dg[1]
-        for d in range(7):
-            pending["z"][d].wait_recv()
-            total = total + gz[d]
-        gx[x] = total
-        diag_send([gx.at[x]] * 3, [gx.at[x]] * 3, [at_x(d) for d in range(1, NX)], 14)
-
-    def diag_share():
-        for d in range(1, NX):
-            src = (x - d) % NX
-            remote(gx.at[src], gx.at[src], dg_s.at[13 + d], dg_r.at[13 + d],
-                   at_x(d)).wait_recv()
-        return diag_send([gx], [gc], [partner], 17)[0]
+            diag_sum(2, pending["x"], gx, 3)
+            pending["c"] = diag_send([dg.at[3]], [gc], [partner], 18)
+        elif t == 3:
+            pending["c"][0].wait_recv()
 
     first = ring(chunk1, q1, r1, s1_s, s1_r, ((y, at_y), (z, at_z)), between1)
+    row_block = (z % 2) * 8 + (y % 2) * 4 + c * 2 + x // 2
+    strip = (x % 2) * 4 + z // 2
+    own_half = (row_block // 8) == c
+    pick = lax.broadcasted_iota(jnp.int32, (8, BLK), 0) == row_block % 8
+    trace = []
+    values = []
+    for f in range(2):
+        a, b = dg[3, f], gc[f]
+        trace.append(jnp.sum(a + b, keepdims=True))
+        chosen = jnp.where(own_half, a, b)
+        values.append(jnp.sum(jnp.where(pick, chosen, 0.0), axis=0, keepdims=True))
+    bound = [jnp.maximum(t, 1e-30) for t in trace]
+    my_bound = jnp.where(par == 0, bound[0], bound[1])
+    to_code = CODE_TOP / my_bound
+    from_code = my_bound / CODE_TOP
+
     second = []
     for d in (4, 3, 5, 2, 6, 1, 7):
         for k in range(2):
@@ -272,26 +293,23 @@
             else:
                 value, dev = pk[(y + d) % NY, z, pl.ds(64, 64), :], at_y(d)
             slot = 7 * k + d - 1
-            encode(value, q2.at[slot])
+            q2[slot] = power(value * to_code).astype(jnp.bfloat16)
             copy = remote(q2.at[slot], r2.at[slot], s2_s.at[slot], s2_r.at[slot], dev)
             copy.start()
             second.append((k, slot, copy))
-    diag_finish()
-    shared = diag_share()
     sums = [pk[y, z, pl.ds(0, 64), :], pk[y, z, pl.ds(64, 64), :]]
     for k, slot, copy in sorted(second, key=lambda e: min(e[1] % 7, 6 - e[1] % 7)):
         copy.wait_recv()
-        sums[k] = sums[k] + decode(r2.at[slot], 64)
-    shared.wait_recv()
-
-    piece = jnp.concatenate(sums, axis=0)
+        sums[k] = sums[k] + root(r2[slot].astype(jnp.float32)) * from_code
+
+    piece = power(jnp.concatenate(sums, axis=0) * to_code)
     flipped = piece.T
     below = (lax.broadcasted_iota(jnp.int32, (BLK, BLK), 0)
              > lax.broadcasted_iota(jnp.int32, (BLK, BLK), 1))
     packed = jnp.logical_and(c == 1, y == z)
     swap = jnp.logical_and(below, packed)
-    outbox[0] = jnp.where(swap, flipped, piece)
-    outbox[1] = jnp.where(swap, piece, flipped)
+    outbox[0] = jnp.where(swap, flipped, piece).astype(jnp.bfloat16)
+    outbox[1] = jnp.where(swap, piece, flipped).astype(jnp.bfloat16)
 
     off_a = jnp.where(y > z, NB, 0)
     off_b = jnp.where(y >= z, NB, 0)
@@ -321,19 +339,6 @@
                 copy.start()
             sends.append((copy, is_me))
 
-    mine = [gx[n] for n in range(NX)]
-    theirs = [gc[n] for n in range(NX)]
-    diag = [(mine[f] + mine[f + 2], theirs[f] + theirs[f + 2]) for f in range(2)]
-    row_block = (z % 2) * 8 + (y % 2) * 4 + c * 2 + x // 2
-    strip = (x % 2) * 4 + z // 2
-    own_half = (row_block // 8) == c
-    pick = lax.broadcasted_iota(jnp.int32, (8, BLK), 0) == row_block % 8
-    trace = []
-    values = []
-    for a, b in diag:
-        trace.append(jnp.sum(a + b, keepdims=True))
-        chosen = jnp.where(own_half, a, b)
-        values.append(jnp.sum(jnp.where(pick, chosen, 0.0), axis=0, keepdims=True))
     ratio = jnp.sqrt(trace[0] / trace[1])
     shift = (ratio * damping, damping / ratio)
     scale = 1.0 / TOKENS
@@ -348,7 +353,9 @@
                 pltpu.make_async_copy(outbox.at[0, pl.ds(0, 16), :], inbox.at[slot],
                                       out_r.at[slot]).wait()
             here = jnp.logical_and(on_diag, (y // 2) * 4 + j == row_block)
-            value = (inbox[8 * f + j] + inbox[8 * f + 4 + j]) * scale
+            value = (root(inbox[8 * f + j].astype(jnp.float32))
+                     + root(inbox[8 * f + 4 + j].astype(jnp.float32)))
+            value = value * (bound[f] * (scale / CODE_TOP))
             out[:, BLK * j:BLK * (j + 1)] = jnp.where(here, damped, value)
 
     for copy, is_me in sends:
@@ -372,30 +379,34 @@
         out_specs=(vmem, vmem),
         scratch_shapes=[
             pltpu.VMEM((4 * ROWS, W), jnp.bfloat16),
+            pltpu.VMEM((ROWS, W), jnp.bfloat16),
             pltpu.VMEM((NB, NB, BLK, BLK), f32),
             pltpu.VMEM((2 * NSLOT, CHUNK + 16, BLK), jnp.bfloat16),
             pltpu.VMEM((2 * NSLOT, CHUNK + 16, BLK), jnp.bfloat16),
-            pltpu.VMEM((14, 80, BLK), jnp.bfloat16),
-            pltpu.VMEM((14, 80, BLK), jnp.bfloat16),
-            pltpu.VMEM((2, BLK, BLK), f32),
-            pltpu.VMEM((16, 16, BLK), f32),
+            pltpu.VMEM((14, 64, BLK), jnp.bfloat16),
+            pltpu.VMEM((14, 64, BLK), jnp.bfloat16),
+            pltpu.VMEM((2, BLK, BLK), jnp.bfloat16),
+            pltpu.VMEM((16, 16, BLK), jnp.bfloat16),
+            pltpu.VMEM((2, 2, 8, BLK), f32),
+            pltpu.VMEM((4, 2, 8, BLK), f32),
+            pltpu.VMEM((1, 2, 8, BLK), f32),
+            pltpu.VMEM((7, 2, 8, BLK), f32),
+            pltpu.VMEM((7, 2, 8, BLK), f32),
+            pltpu.VMEM((3, 2, 8, BLK), f32),
             pltpu.VMEM((2, 8, BLK), f32),
-            pltpu.VMEM((7, 8, BLK), f32),
-            pltpu.VMEM((7, 8, BLK), f32),
-            pltpu.VMEM((NX, 8, BLK), f32),
-            pltpu.VMEM((NX, 8, BLK), f32),
-            dma,
+            dma((2,)),
             dma((4 * RAW + 1,)), dma((4 * RAW + 1,)),
             dma((2 * NSLOT,)), dma((2 * NSLOT,)),
             dma((2 * NSLOT,)), dma((2 * NSLOT,)),
-            dma((18,)), dma((18,)),
+            dma((19,)), dma((19,)),
             dma((16,)), dma((16,)),
         ],
         compiler_params=pltpu.CompilerParams(
             collective_id=0, has_side_effects=True,
-            vmem_limit_bytes=62 * 1024 * 1024),
+            vmem_limit_bytes=48 * 1024 * 1024),
         name="kfac",
-    )(act_input, out_grad)
+    )(pltpu.with_memory_space_constraint(act_input, pltpu.HBM),
+      pltpu.with_memory_space_constraint(out_grad, pltpu.HBM))
     return act_out[None, None], grad_out[None, None]
 
 

time: 63.2 us -> 57.8 us (0.915)
  the two profiles are of different devices: /device:TPU:31 before, /device:TPU:49 now
where the time goes in v5:
time: 57.8 us; the launch traced here: 57.7 us
  Pallas kernels  55.8 us (97%)
  local copies, waits for them, and re-layouts  1.23 us (2%)
  between operations  0.64 us (1%)
    pallas_call x1, Pallas kernels, on_device(): pl.pallas_call(kernel, out_shape=(piece, piece), in_specs=[any_space, any...  55.8 us
    unnamed x2, local copies, waits for them, and re-layouts  1.23 us

profile of v5, /device:TPU:49, one launch (start us, length us, event | category | flops | bytes accessed | tf_op | source)
XLA Modules:
  0.0 57.7 jit_solution(13943234697241804688)
XLA Ops:
  0.6 55.8 %kfac.1 = (f32[16,512]{1,0:T(8,128)S(1)}, f32[16,512]{1,0:T(8,128)S(1)}) custom-call(bf16[160,2048]{1,0:T(8,128)(2,1)} %act.1, bf16[160,2048]{1,0:T(8,128)(2,1)} %grad.1), custom_call_target="tpu_custom_call" | custom-call | tf_op jit(solution)/shard_map/kfac/pallas_call | solution.py:375
  56.4 0.6 %copy.6 = f32[1,1,16,512]{3,2,1,0:T(8,128)} copy(f32[1,1,16,512]{3,2,1,0:T(8,128)S(1)} %bitcast.3) | data formatting | bytes 65536
  57.0 0.6 %copy.7 = f32[1,1,16,512]{3,2,1,0:T(8,128)} copy(f32[1,1,16,512]{3,2,1,0:T(8,128)S(1)} %bitcast.2) | data formatting | bytes 65536

commit v6 on v5

--- a/solution.py
+++ b/solution.py
@@ -21,7 +21,7 @@
            (1, 1, 3), (0, -1, 3), (3, 1, 3), (2, -1, 3))
 BASE = (0, 4, 8, 12, 16, 19, 22, 25)
 NSLOT = 28
-RAW = 2
+RAW = 4
 CHUNK = 128
 CODE_TOP = 2.0 ** 15
 
@@ -32,7 +32,7 @@
 
 def kernel(act, grad, act_out, grad_out,
            xb, ob, pk, q1, r1, q2, r2, outbox, inbox, dl, dg, gd, gy, gz, gx, gc,
-           loc_sem, raw_s, raw_r, s1_s, s1_r, s2_s, s2_r,
+           near, loc_sem, raw_s, raw_r, s1_s, s1_r, s2_s, s2_r,
            dg_s, dg_r, out_s, out_r):
     dp = lax.axis_index("dp")
     ctx = lax.axis_index("ctx")
@@ -59,8 +59,8 @@
             device_id=dev, device_id_type=MESH)
 
     barrier = pltpu.get_barrier_semaphore()
-    peers = [partner] + [at_x(d) for d in range(1, NX)]
-    peers += [at_y(d) for d in range(1, NY)] + [at_z(d) for d in range(1, NZ)]
+    around = [at_y(1), at_y(-1), at_z(1), at_z(-1)]
+    peers = [partner, at_x(1), at_x(-1)] + around
     for dev in peers:
         pl.semaphore_signal(barrier, inc=1, device_id=dev, device_id_type=MESH)
 
@@ -104,6 +104,14 @@
         for copy in raw_copies(grad, act):
             copy.start()
 
+    def tell(n):
+        for dev in around:
+            pl.semaphore_signal(near.at[n], inc=1, device_id=dev, device_id_type=MESH)
+
+    def hear(n):
+        pl.semaphore_wait(near.at[n], len(around))
+
+    tell(0)
     raw = raw_copies(act, grad)
     pltpu.make_async_copy(act, own_rows, loc_sem.at[0]).wait()
     pltpu.make_async_copy(act, ob, loc_sem.at[1]).wait()
@@ -131,6 +139,8 @@
             part = tokens[:, BLK * i:BLK * (i + 1)].astype(jnp.float32)
             dl[i // NB, f, pl.ds(i % NB, 1), :] = jnp.sum(part * part, axis=0, keepdims=True)
     pending = {"d": diag_send([dl.at[1 - c]], [gd.at[0]], [partner], 0)}
+    hear(0)
+    tell(1)
     raw[2 * RAW].wait_recv()
 
     contract = (((0,), (0,)), ((), ()))
@@ -175,10 +185,13 @@
                     else:
                         store(a, b, jnp.where(upper, high, low), add)
 
+    hear(1)
+    tell(2)
     tile_grid(0, False)
 
     dg[0] = dl[c]
     diag_sum(0, pending["d"], gd, 0)
+    hear(2)
     pending["y"] = diag_send([dg.at[0]] * 7, [gy.at[d - 1] for d in range(1, NY)],
                              [at_y(d) for d in range(1, NY)], 1)
 
@@ -394,6 +407,7 @@
             pltpu.VMEM((7, 2, 8, BLK), f32),
             pltpu.VMEM((3, 2, 8, BLK), f32),
             pltpu.VMEM((2, 8, BLK), f32),
+            pltpu.SemaphoreType.REGULAR((3,)),
             dma((2,)),
             dma((4 * RAW + 1,)), dma((4 * RAW + 1,)),
             dma((2 * NSLOT,)), dma((2 * NSLOT,)),

time: 57.8 us -> 56.7 us (0.981)
  Pallas kernels: 55.8 us -> 54.7 us
    pallas_call x1, Pallas kernels: 55.8 us -> 54.7 us  [on_device(): pl.pallas_call(kernel, out_shape=(piece, piece), in_specs=[any_space, any...]
where the time goes in v6:
time: 56.7 us; the launch traced here: 56.5 us
  Pallas kernels  54.7 us (96%)
  local copies, waits for them, and re-layouts  1.23 us (2%)
  between operations  0.64 us (1%)
    pallas_call x1, Pallas kernels, on_device(): pl.pallas_call(kernel, out_shape=(piece, piece), in_specs=[any_space, any...  54.7 us
    unnamed x2, local copies, waits for them, and re-layouts  1.23 us

profile of v6, /device:TPU:49, one launch (start us, length us, event | category | flops | bytes accessed | tf_op | source)
XLA Modules:
  0.0 56.5 jit_solution(3000311676560149075)
XLA Ops:
  0.6 54.7 %kfac.1 = (f32[16,512]{1,0:T(8,128)S(1)}, f32[16,512]{1,0:T(8,128)S(1)}) custom-call(bf16[160,2048]{1,0:T(8,128)(2,1)} %act.1, bf16[160,2048]{1,0:T(8,128)(2,1)} %grad.1), custom_call_target="tpu_custom_call" | custom-call | tf_op jit(solution)/shard_map/kfac/pallas_call | solution.py:388
  55.3 0.6 %copy.6 = f32[1,1,16,512]{3,2,1,0:T(8,128)} copy(f32[1,1,16,512]{3,2,1,0:T(8,128)S(1)} %bitcast.3) | data formatting | bytes 65536
  55.9 0.6 %copy.7 = f32[1,1,16,512]{3,2,1,0:T(8,128)} copy(f32[1,1,16,512]{3,2,1,0:T(8,128)S(1)} %bitcast.2) | data formatting | bytes 65536

commit v7 on v6

--- a/solution.py
+++ b/solution.py
@@ -30,7 +30,7 @@
     return (x * (NZ // 2) + z // 2, (z % 2) * (2 * NY) + y * 2 + c)
 
 
-def kernel(act, grad, act_out, grad_out,
+def kernel(act, grad, outs,
            xb, ob, pk, q1, r1, q2, r2, outbox, inbox, dl, dg, gd, gy, gz, gx, gc,
            near, loc_sem, raw_s, raw_r, s1_s, s1_r, s2_s, s2_r,
            dg_s, dg_r, out_s, out_r):
@@ -358,7 +358,6 @@
     on_diag = (lax.broadcasted_iota(jnp.int32, (16, BLK), 1)
                == lax.broadcasted_iota(jnp.int32, (16, BLK), 0) + 16 * strip)
     for f in range(2):
-        out = (act_out, grad_out)[f]
         damped = values[f] * scale + shift[f]
         for j in range(4):
             for n in range(2):
@@ -369,7 +368,7 @@
             value = (root(inbox[8 * f + j].astype(jnp.float32))
                      + root(inbox[8 * f + 4 + j].astype(jnp.float32)))
             value = value * (bound[f] * (scale / CODE_TOP))
-            out[:, BLK * j:BLK * (j + 1)] = jnp.where(here, damped, value)
+            outs[f, :, BLK * j:BLK * (j + 1)] = jnp.where(here, damped, value)
 
     for copy, is_me in sends:
         @pl.when(jnp.logical_not(is_me))
@@ -381,15 +380,15 @@
 
 def on_device(act_input, out_grad):
     f32 = jnp.float32
-    piece = jax.ShapeDtypeStruct((16, 4 * BLK), f32)
+    piece = jax.ShapeDtypeStruct((2, 16, 4 * BLK), f32)
     any_space = pl.BlockSpec(memory_space=pltpu.HBM)
     vmem = pl.BlockSpec(memory_space=pltpu.VMEM)
     dma = pltpu.SemaphoreType.DMA
-    act_out, grad_out = pl.pallas_call(
+    outs = pl.pallas_call(
         kernel,
-        out_shape=(piece, piece),
+        out_shape=piece,
         in_specs=[any_space, any_space],
-        out_specs=(vmem, vmem),
+        out_specs=vmem,
         scratch_shapes=[
             pltpu.VMEM((4 * ROWS, W), jnp.bfloat16),
             pltpu.VMEM((ROWS, W), jnp.bfloat16),
@@ -421,7 +420,7 @@
         name="kfac",
     )(pltpu.with_memory_space_constraint(act_input, pltpu.HBM),
       pltpu.with_memory_space_constraint(out_grad, pltpu.HBM))
-    return act_out[None, None], grad_out[None, None]
+    return outs[0][None, None], outs[1][None, None]
 
 
 def solution(mesh):

time: 56.7 us -> 56.1 us (0.989)
  local copies, waits for them, and re-layouts: 1.23 us -> 0.63 us
    unnamed x2 -> x0, local copies, waits for them, and re-layouts: 1.23 us -> none
    another operation x0 -> x1, local copies, waits for them, and re-layouts: none -> 0.63 us  [on_device(): return (outs[0][None, None], outs[1][None, None])]
where the time goes in v7:
time: 56.1 us; the launch traced here: 55.9 us
  Pallas kernels  54.7 us (98%)
  between operations  0.64 us (1%)
  local copies, waits for them, and re-layouts  0.63 us (1%)
    pallas_call x1, Pallas kernels, on_device(): pl.pallas_call(kernel, out_shape=piece, in_specs=[any_space, any_space],...  54.7 us

profile of v7, /device:TPU:49, one launch (start us, length us, event | category | flops | bytes accessed | tf_op | source)
XLA Modules:
  0.0 55.9 jit_solution(15913426751485352283)
XLA Ops:
  0.6 54.7 %kfac.1 = f32[2,16,512]{2,1,0:T(8,128)S(1)} custom-call(bf16[160,2048]{1,0:T(8,128)(2,1)} %act.1, bf16[160,2048]{1,0:T(8,128)(2,1)} %grad.1), custom_call_target="tpu_custom_call" | custom-call | tf_op jit(solution)/shard_map/kfac/pallas_call | solution.py:387
  55.3 0.6 %slice_bitcast_fusion = (f32[1,1,16,512]{3,2,1,0:T(8,128)}, f32[1,1,16,512]{3,2,1,0:T(8,128)}) fusion(f32[2,16,512]{2,1,0:T(8,128)S(1)} %kfac.1), kind=kLoop, calls=%fused_computation | loop fusion | bytes 131072 | tf_op jit(solution)/shard_map/broadcast_in_dim;squeeze | solution.py:423
